TPU v7x, 128 devices: a whole 4x4x4 slice. The times are simulated.
128 devices in a mesh: region: 32 (over y, z, x_lo), col: 4 (over x_hi, core).
Axes of the slice: x: 4 (x_hi: 2, x_lo: 2; x = x_hi * 2 + x_lo), y: 4, z: 4, core: 2. Of those that a mesh axis runs over, the one named last changes fastest.
Arguments:
- basis_v: bfloat16 [196608, 512], P('region', 'col'), may hold values from -6 to 6
- basis_w: bfloat16 [196608, 512], P(('region', 'col')), may hold values from -0.0546875 to 0.0546875
- couplings: bfloat16 [1536, 48, 128, 128], P('region', 'col'), may hold values from -0.078125 to 0.078125
- coupling_cols: int32 [1536, 48], P('region', 'col'), may hold values from 0 to 1535, as said below
Outputs:
- reduced: float32 [512, 512], P(('region', 'col'))
Inputs may be any that keep to these rules, and one draw needn't show every extreme that they name: `coupling_cols`: the 48 block columns of one block row are distinct and differ from its row number by at most 48; every block row takes the columns at distance 48 on both sides where they exist.
All inputs are finite; a program needn't handle non-finite values.
Results may differ from a plain program's by a relative error of at most 0.0003.
Values may be sent and summed in bfloat16 or wider, within the bound.
A program may use at most 192 MiB of HBM per device.

v0:
```python
import math

import jax
import jax.numpy as jnp
from jax import lax
from jax.sharding import PartitionSpec as P


def extended(block, sides, width):
    for axis, dim in sides:
        count = lax.axis_size(axis)
        forward = [(i, i + 1) for i in range(count - 1)]
        backward = [(target, source) for source, target in forward]
        low = lax.ppermute(
            lax.slice_in_dim(block, block.shape[dim] - width, None, axis=dim), axis, forward
        )
        high = lax.ppermute(lax.slice_in_dim(block, 0, width, axis=dim), axis, backward)
        block = jnp.concatenate([low, block, high], axis=dim)
    return block


def coupled_rows(couplings, local_cols, widened_blocks, length):
    block = couplings.shape[2]
    slots_here = couplings.shape[1]
    width = widened_blocks.shape[2]
    per_group = math.gcd(length, 8)
    a_part = couplings
    c_part = local_cols
    a_part = a_part.reshape(length // per_group, per_group, slots_here, block, block)
    c_part = c_part.reshape(length // per_group, per_group, slots_here)

    def one_group(operands):
        blocks, columns = operands
        picked = widened_blocks[columns]
        return jnp.einsum("gkrs,gksc->grc", blocks, picked, preferred_element_type=jnp.float32)

    results = lax.map(one_group, (a_part, c_part))
    return results.reshape(length * block, width)


def project_rows(w_rows, image_rows):
    upper_part = image_rows.astype(jnp.bfloat16)
    kept_upper = lax.optimization_barrier(upper_part)
    lower_part = (image_rows - kept_upper.astype(jnp.float32)).astype(jnp.bfloat16)
    first_term = jnp.einsum("rc,rd->cd", w_rows, upper_part, preferred_element_type=jnp.float32)
    second_term = jnp.einsum("rc,rd->cd", w_rows, lower_part, preferred_element_type=jnp.float32)
    return first_term + second_term


def shards(basis_v, basis_w, couplings, coupling_cols):
    blocks_dev = couplings.shape[0]
    block = couplings.shape[2]
    rows_dev = blocks_dev * block
    region = lax.axis_index("region")
    all_columns = lax.all_gather(basis_v, "col", axis=1, tiled=True)
    widened = extended(all_columns, (("region", 0),), rows_dev)
    width = widened.shape[1]
    widened_blocks = widened.reshape(3 * blocks_dev, block, width)
    local_cols = coupling_cols - (region * blocks_dev - blocks_dev)

    def image_rows(offset, length):
        return coupled_rows(couplings, local_cols, widened_blocks, length // block)

    coupled_image = lax.psum_scatter(
        image_rows(jnp.int32(0), rows_dev // lax.axis_size("col") * lax.axis_size("col")),
        "col",
        scatter_dimension=0,
        tiled=True,
    )
    partial_tile = project_rows(basis_w, coupled_image)
    return lax.psum_scatter(partial_tile, ("region", "col"), scatter_dimension=0, tiled=True)


def solution(mesh):
    in_specs = (
        P("region", "col"),
        P(("region", "col"), None),
        P("region", "col", None, None),
        P("region", "col"),
    )
    out_specs = P(("region", "col"), None)
    return jax.shard_map(shards, mesh=mesh, in_specs=in_specs, out_specs=out_specs, check_vma=False)
```

profile of v0, /device:TPU:1, one launch (start us, length us, event | category | flops | bytes accessed | tf_op | source)
XLA Modules:
  0.0 762.0 jit_solution(17104147953014549866)
XLA Ops:
  6.5 0.7 all-gather.2.cloned.1.call-update
  7.3 56.5 %all-gather.2.cloned.1.call-done = bf16[6144,512]{1,0:T(8,128)(2,1)} async-done(((bf16[6144,128]{1,0:T(8,128)(2,1)}), bf16[6144,512]{1,0:T(8,128)(2,1)}) %all-gather.2.cloned.1.call-update) | async-done | bytes 6291472 | tf_op jit(solution)/shard_map/all_gather | solution.py:55
  63.8 4.8 collective-permute-start
  68.6 1.3 collective-permute-start.1
  69.9 0.7 broadcast_subtract_fusion
  70.6 0.1 copy.7
  70.7 130.2 %collective-permute-done = bf16[6144,512]{1,0:T(8,128)(2,1)} collective-permute-done((bf16[6144,512]{1,0:T(8,128)(2,1)}, bf16[6144,512]{1,0:T(8,128)(2,1)}, u32[]{:S(2)}, u32[]{:S(2)}) %collective-permute-start) | collective-permute-done | bytes 6291488 | tf_op jit(solution)/shard_map/ppermute | solution.py:14
  200.9 137.7 %collective-permute-done.1 = bf16[6144,512]{1,0:T(8,128)(2,1)} collective-permute-done((bf16[6144,512]{1,0:T(8,128)(2,1)}, bf16[6144,512]{1,0:T(8,128)(2,1)}, u32[]{:S(2)}, u32[]{:S(2)}) %collective-permute-start.1) | collective-permute-done | bytes 6291488 | tf_op jit(solution)/shard_map/ppermute | solution.py:17
  338.7 21.4 %pad_maximum_fusion = bf16[18432,512]{1,0:T(8,128)(2,1)} fusion(bf16[6144,512]{1,0:T(8,128)(2,1)} %collective-permute-done.1, bf16[6144,512]{1,0:T(8,128)(2,1)} %all-gather.2.cloned.1.call-done, bf16[6144,512]{1,0:T(8,128)(2,1)} %collective-permute-done), kind=kLoop, calls=%fused_computation.8 | loop fusion | flops 56623104 | bytes 37748736 | tf_op jit(solution)/shard_map/concatenate | solution.py:18
  360.1 132.3 %while.10 = (s32[]{:T(128)}, f32[6,8,128,512]{3,2,1,0:T(8,128)}, bf16[6,8,12,128,128]{4,3,2,1,0:T(8,128)(2,1)}, s32[6,8,12]{2,1,0:T(8,128)S(1)}, bf16[144,128,512]{2,1,0:T(8,128)(2,1)}, /*index=5*/s32[]{:T(128)}) while((s32[]{:T(128)}, f32[6,8,128,512]{3,2,1,0:T(8,128)}, bf16[6,8,12,128,128]{4,3,2,1,0:T(8,128)(2,1)}, ...), condition=%wide.region_1.2_spmd, body=%wide.region_0.1_spmd.sunk | while | flops 1610614016 | bytes 42999112 | solution.py:37
  360.2 13.3 %gather_fusion = bf16[96,128,512]{2,1,0:T(8,128)(2,1)} fusion(bf16[144,128,512]{2,1,0:T(8,128)(2,1)} %get-tuple-element.90, s32[1024]{0:T(1024)S(1)} %pad_clamp_fusion.2), kind=kCustom, calls=%fused_computation.clone.1 | custom fusion | bytes 25166208 | tf_op jit(solution)/shard_map/while/body/eval_jaxpr/gather | solution.py:34
  373.5 8.7 %bitcast_dynamic-update-slice_fusion.2 = f32[6,8,128,512]{3,2,1,0:T(8,128)} fusion(f32[6,8,128,512]{3,2,1,0:T(8,128)} %get-tuple-element.81, s32[]{:T(128)} %get-tuple-element.80, bf16[8,12,128,512]{3,2,1,0:T(8,128)(2,1)} %bitcast.36, bf16[6,8,12,128,128]{4,3,2,1,0:T(8,128)(2,1)} %get-tuple-element.88), kind=kOutput, calls=%fused_computation.4.clone.1 | convolution fusion | flops 1610612736 | bytes 17826816 | tf_op jit(solution)/shard_map/while/body/eval_jaxpr/gkrs,gksc->grc/dot_general | solution.py:35
  382.1 0.1 reshape.61
  382.2 13.3 %gather_fusion = bf16[96,128,512]{2,1,0:T(8,128)(2,1)} fusion(bf16[144,128,512]{2,1,0:T(8,128)(2,1)} %get-tuple-element.90, s32[1024]{0:T(1024)S(1)} %pad_clamp_fusion.2), kind=kCustom, calls=%fused_computation.clone.1 | custom fusion | bytes 25166208 | tf_op jit(solution)/shard_map/while/body/eval_jaxpr/gather | solution.py:34
  395.5 8.7 %bitcast_dynamic-update-slice_fusion.2 = f32[6,8,128,512]{3,2,1,0:T(8,128)} fusion(f32[6,8,128,512]{3,2,1,0:T(8,128)} %get-tuple-element.81, s32[]{:T(128)} %get-tuple-element.80, bf16[8,12,128,512]{3,2,1,0:T(8,128)(2,1)} %bitcast.36, bf16[6,8,12,128,128]{4,3,2,1,0:T(8,128)(2,1)} %get-tuple-element.88), kind=kOutput, calls=%fused_computation.4.clone.1 | convolution fusion | flops 1610612736 | bytes 17826816 | tf_op jit(solution)/shard_map/while/body/eval_jaxpr/gkrs,gksc->grc/dot_general | solution.py:35
  404.2 0.1 reshape.61
  404.3 13.3 %gather_fusion = bf16[96,128,512]{2,1,0:T(8,128)(2,1)} fusion(bf16[144,128,512]{2,1,0:T(8,128)(2,1)} %get-tuple-element.90, s32[1024]{0:T(1024)S(1)} %pad_clamp_fusion.2), kind=kCustom, calls=%fused_computation.clone.1 | custom fusion | bytes 25166208 | tf_op jit(solution)/shard_map/while/body/eval_jaxpr/gather | solution.py:34
  417.5 8.7 %bitcast_dynamic-update-slice_fusion.2 = f32[6,8,128,512]{3,2,1,0:T(8,128)} fusion(f32[6,8,128,512]{3,2,1,0:T(8,128)} %get-tuple-element.81, s32[]{:T(128)} %get-tuple-element.80, bf16[8,12,128,512]{3,2,1,0:T(8,128)(2,1)} %bitcast.36, bf16[6,8,12,128,128]{4,3,2,1,0:T(8,128)(2,1)} %get-tuple-element.88), kind=kOutput, calls=%fused_computation.4.clone.1 | convolution fusion | flops 1610612736 | bytes 17826816 | tf_op jit(solution)/shard_map/while/body/eval_jaxpr/gkrs,gksc->grc/dot_general | solution.py:35
  426.2 0.1 reshape.61
  426.3 13.3 %gather_fusion = bf16[96,128,512]{2,1,0:T(8,128)(2,1)} fusion(bf16[144,128,512]{2,1,0:T(8,128)(2,1)} %get-tuple-element.90, s32[1024]{0:T(1024)S(1)} %pad_clamp_fusion.2), kind=kCustom, calls=%fused_computation.clone.1 | custom fusion | bytes 25166208 | tf_op jit(solution)/shard_map/while/body/eval_jaxpr/gather | solution.py:34
  439.6 8.7 %bitcast_dynamic-update-slice_fusion.2 = f32[6,8,128,512]{3,2,1,0:T(8,128)} fusion(f32[6,8,128,512]{3,2,1,0:T(8,128)} %get-tuple-element.81, s32[]{:T(128)} %get-tuple-element.80, bf16[8,12,128,512]{3,2,1,0:T(8,128)(2,1)} %bitcast.36, bf16[6,8,12,128,128]{4,3,2,1,0:T(8,128)(2,1)} %get-tuple-element.88), kind=kOutput, calls=%fused_computation.4.clone.1 | convolution fusion | flops 1610612736 | bytes 17826816 | tf_op jit(solution)/shard_map/while/body/eval_jaxpr/gkrs,gksc->grc/dot_general | solution.py:35
  448.4 13.3 %gather_fusion = bf16[96,128,512]{2,1,0:T(8,128)(2,1)} fusion(bf16[144,128,512]{2,1,0:T(8,128)(2,1)} %get-tuple-element.90, s32[1024]{0:T(1024)S(1)} %pad_clamp_fusion.2), kind=kCustom, calls=%fused_computation.clone.1 | custom fusion | bytes 25166208 | tf_op jit(solution)/shard_map/while/body/eval_jaxpr/gather | solution.py:34
  461.7 8.7 %bitcast_dynamic-update-slice_fusion.2 = f32[6,8,128,512]{3,2,1,0:T(8,128)} fusion(f32[6,8,128,512]{3,2,1,0:T(8,128)} %get-tuple-element.81, s32[]{:T(128)} %get-tuple-element.80, bf16[8,12,128,512]{3,2,1,0:T(8,128)(2,1)} %bitcast.36, bf16[6,8,12,128,128]{4,3,2,1,0:T(8,128)(2,1)} %get-tuple-element.88), kind=kOutput, calls=%fused_computation.4.clone.1 | convolution fusion | flops 1610612736 | bytes 17826816 | tf_op jit(solution)/shard_map/while/body/eval_jaxpr/gkrs,gksc->grc/dot_general | solution.py:35
  470.4 13.3 %gather_fusion = bf16[96,128,512]{2,1,0:T(8,128)(2,1)} fusion(bf16[144,128,512]{2,1,0:T(8,128)(2,1)} %get-tuple-element.90, s32[1024]{0:T(1024)S(1)} %pad_clamp_fusion.2), kind=kCustom, calls=%fused_computation.clone.1 | custom fusion | bytes 25166208 | tf_op jit(solution)/shard_map/while/body/eval_jaxpr/gather | solution.py:34
  483.7 8.7 %bitcast_dynamic-update-slice_fusion.2 = f32[6,8,128,512]{3,2,1,0:T(8,128)} fusion(f32[6,8,128,512]{3,2,1,0:T(8,128)} %get-tuple-element.81, s32[]{:T(128)} %get-tuple-element.80, bf16[8,12,128,512]{3,2,1,0:T(8,128)(2,1)} %bitcast.36, bf16[6,8,12,128,128]{4,3,2,1,0:T(8,128)(2,1)} %get-tuple-element.88), kind=kOutput, calls=%fused_computation.4.clone.1 | convolution fusion | flops 1610612736 | bytes 17826816 | tf_op jit(solution)/shard_map/while/body/eval_jaxpr/gkrs,gksc->grc/dot_general | solution.py:35
  492.5 106.0 %reduce-scatter.3.cloned.1.call-done = f32[1536,512]{1,0:T(8,128)} async-done(((f32[6144,512]{1,0:T(8,128)}), f32[1536,512]{1,0:T(8,128)}) %reduce-scatter.3.cloned.1.call-update) | async-done | bytes 3145744 | tf_op jit(solution)/shard_map/reduce_scatter | solution.py:64
  598.5 2.1 convert_element_type.9
  600.6 2.9 fusion.6
  603.6 2.0 fusion.7
  605.6 148.1 %all-reduce.3.cloned.1.call-done = f32[512,512]{0,1:T(8,128)} async-done(((f32[512,512]{0,1:T(8,128)}), f32[512,512]{0,1:T(8,128)}) %all-reduce.3.cloned.1.call-update) | async-done | bytes 1048592
  753.7 1.1 constant_dynamic-slice_fusion
  754.8 0.7 copy.8
  (23 shorter events, 0.4 us)
Async XLA Ops:
  6.5 594.1 %copy-start = (bf16[1536,512]{1,0:T(8,128)(2,1)S(1)}, bf16[1536,512]{1,0:T(8,128)(2,1)}, u32[]{:S(2)}) copy-start(bf16[1536,512]{1,0:T(8,128)(2,1)} %param.7) | copy-start | bytes 4718596
  6.5 57.3 %all-gather.2.cloned.1.call-start = ((), (), s32[]{:S(2)}) async-start(), calls=%async_computation.1 | async-start | bytes 7864320 | tf_op jit(solution)/shard_map/all_gather | solution.py:55
  7.3 591.3 %reduce-scatter.3.cloned.1.call-start = ((), (), s32[]{:S(2)}) async-start(), calls=%async_computation.2 | async-start | bytes 15728640 | tf_op jit(solution)/shard_map/reduce_scatter | solution.py:64
  63.8 137.1 %collective-permute-start = (bf16[6144,512]{1,0:T(8,128)(2,1)}, bf16[6144,512]{1,0:T(8,128)(2,1)}, u32[]{:S(2)}, u32[]{:S(2)}) collective-permute-start(bf16[6144,512]{1,0:T(8,128)(2,1)} %all-gather.2.cloned.1.call-done), channel_id=1, source_target_pairs={{0,4},{4,8},{8,12},{12,16},{16,20},{20,24},{24,28},{28,32},{32,36}... | collective-permute-start | bytes 18874376 | tf_op jit(solution)/shard_map/ppermute | solution.py:14
  68.6 270.1 %collective-permute-start.1 = (bf16[6144,512]{1,0:T(8,128)(2,1)}, bf16[6144,512]{1,0:T(8,128)(2,1)}, u32[]{:S(2)}, u32[]{:S(2)}) collective-permute-start(bf16[6144,512]{1,0:T(8,128)(2,1)} %all-gather.2.cloned.1.call-done), channel_id=1, source_target_pairs={{4,0},{8,4},{12,8},{16,12},{20,16},{24,20},{28,24},{32,28},{36,32}... | collective-permute-start | bytes 18874376 | tf_op jit(solution)/shard_map/ppermute | solution.py:17
  492.4 261.3 %all-reduce.3.cloned.1.call-start = ((), (), s32[]{:S(2)}) async-start(), calls=%async_computation.3 | async-start | bytes 2097152
Sparse Core Ops, SparseCore 0:
  9.0 54.8 all-gather.1
  492.5 105.9 reduce-scatter.2
  605.7 147.9 all-reduce.2
where the time goes:
time: 763 us; the launch traced here: 762 us
  waiting for transfers between devices  579 us (76%)
  local copies, waits for them, and re-layouts  82 us (11%)
  matrix products  57.1 us (7%)
  other arithmetic  24.3 us (3%)
  between operations  13.2 us (2%)
    unnamed x4, waiting for transfers between devices  149 us
    ppermute x1, waiting for transfers between devices, extended(): lax.ppermute(lax.slice_in_dim(block, 0, width, axis=dim), axis, backward)  138 us
    ppermute x1, waiting for transfers between devices, extended(): lax.ppermute(lax.slice_in_dim(block, block.shape[dim] - width, None, axis...  130 us
    reduce_scatter x1, waiting for transfers between devices, shards(): lax.psum_scatter(image_rows(jnp.int32(0), rows_dev // lax.axis_size('col'...  106 us
    gather x6, local copies, waits for them, and re-layouts, one_group(): picked = widened_blocks[columns]  79.6 us
    all_gather x1, waiting for transfers between devices, shards(): all_columns = lax.all_gather(basis_v, 'col', axis=1, tiled=True)  56.5 us
    dot_general x6, matrix products, one_group(): jnp.einsum('gkrs,gksc->grc', blocks, picked, preferred_element_type=jnp.f...  52.1 us
    concatenate x1, other arithmetic, extended(): block = jnp.concatenate([low, block, high], axis=dim)  21.4 us
  transfers between devices with their start and end apart: 5, of which 5 were waited for; matrix products, arithmetic and copies ran while one was open for 0% of the time, Pallas kernels for 0%

commit v1 on v0

v1 whole, which is shorter than its diff:
```python
import functools

import jax
import jax.numpy as jnp
from jax import lax
from jax.experimental import pallas as pl
from jax.experimental.pallas import tpu as pltpu
from jax.sharding import PartitionSpec as P

MESH = pl.DeviceIdType.MESH
CHUNKS = 8
HALF_CHUNKS = 2


def kernel(
    regions, cols_ref, a_hbm, v_hbm, w_hbm, o_ref,
    a, v, w, wr, hi, lo, acc, r0, t1, t2, rx, ry, u1, u2, r2x, r2y, fin, rf,
    loc, vs, vr, bs, br, ws, wrecv, qs_sem, qr_sem,
):
    nb, slots = a.shape[0], a.shape[1]
    n, half = CHUNKS, CHUNKS // 2
    cb = nb // n
    wb = w.shape[1]
    wh = wb // (2 * HALF_CHUNKS)
    pairs = regions // 2
    basis = acc.shape[-1]
    quarter = basis // 4

    r, q = lax.axis_index("region"), lax.axis_index("col")
    par, core, xh = r % 2, q % 2, q // 2
    k = r // 2
    q2 = (q + 2) % 4
    qs = q + 1 - 2 * core
    qs2 = (qs + 2) % 4
    partner = r + 1 - 2 * par
    dev_a = (partner, q)
    dev_b = (partner, q2)
    dev_d = (r, q2)
    dev_s = (r, qs)
    dev_z = ((r + 2 - 4 * par + regions) % regions, q)
    others = [(((k + j) % pairs) * 2 + par, q) for j in range(1, pairs)]
    here = nb
    near = 2 * nb * (1 - par)
    far = 2 * nb * par

    get_a = pltpu.make_async_copy(a_hbm, a, loc.at[0])
    get_v = pltpu.make_async_copy(v_hbm, v.at[q, pl.ds(here, nb)], loc.at[1])
    get_w = pltpu.make_async_copy(w_hbm, w.at[q], loc.at[2])
    get_v.start()
    get_w.start()

    barrier = pltpu.get_barrier_semaphore()
    greeted = [dev_a, dev_b, dev_d, dev_s] + others
    for dev in greeted:
        pl.semaphore_signal(barrier, inc=1, device_id=dev, device_id_type=MESH)
    pl.semaphore_wait(barrier, len(greeted))

    sent = []

    def send(src, dst, ssem, rsem, dev):
        copy = pltpu.make_async_remote_copy(
            src_ref=src, dst_ref=dst, send_sem=ssem, recv_sem=rsem,
            device_id=dev, device_id_type=MESH,
        )
        copy.start()
        sent.append(copy)

    def arrived(dst, rsem):
        pltpu.make_async_copy(dst, dst, rsem).wait()

    def piece(col, base, c):
        return v.at[col, pl.ds(base + c * cb, cb)]

    for t in range(n):
        c = t
        send(v_hbm.at[pl.ds(c * cb, cb)], piece(q, far, c), vs.at[0, c], vr.at[0, c], dev_a)
        c = (t + half) % n
        send(v_hbm.at[pl.ds(c * cb, cb)], piece(q, far, c), vs.at[1, c], vr.at[1, c], dev_b)
    send(v_hbm, v.at[q, pl.ds(here, nb)], bs.at[0, 0], br.at[0, 0], dev_s)
    send(w_hbm, w.at[q], ws.at[0], wrecv.at[0], dev_s)
    get_a.start()

    def to_sibling(slab, col, base, c):
        ref = piece(col, base, c)
        send(ref, ref, bs.at[slab, c], br.at[slab, c], dev_s)

    def take_a(c):
        arrived(piece(q, near, c), vr.at[0, c])
        src = piece(q, near, c)
        send(src, piece(q, far, c), vs.at[3, c], vr.at[3, c], dev_z)
        if c < half:
            send(src, piece(q, here, c), vs.at[2, c], vr.at[2, c], dev_b)
        to_sibling(1, q, near, c)

    def take_b(c):
        arrived(piece(q2, near, c), vr.at[1, c])
        src = piece(q2, near, c)
        send(src, piece(q2, far, c), vs.at[4, c], vr.at[4, c], dev_z)
        if c >= half:
            send(src, piece(q2, here, c), vs.at[2, c], vr.at[2, c], dev_a)
        to_sibling(2, q2, near, c)

    def take_d(c):
        arrived(piece(q2, here, c), vr.at[2, c])
        to_sibling(3, q2, here, c)

    def take_z(j):
        c = j // 2
        if j % 2 == 0:
            arrived(piece(q, far, c), vr.at[3, c])
            to_sibling(4, q, far, c)
        else:
            c = (c + half) % n
            arrived(piece(q2, far, c), vr.at[4, c])
            to_sibling(5, q2, far, c)

    for t in range(n):
        take_a(t)
        take_b((t + half) % n)

    for h in range(HALF_CHUNKS):
        send(w_hbm.at[pl.ds(h * wh, wh)], wr.at[0, h], ws.at[1 + h], wrecv.at[1 + h], dev_a)
        o = 1 + HALF_CHUNKS + h
        send(w_hbm.at[pl.ds(wb // 2 + h * wh, wh)], wr.at[1, h], ws.at[o], wrecv.at[o], dev_b)

    def relay_w(h):
        o = 1 + 2 * HALF_CHUNKS + h
        arrived(wr.at[0, h], wrecv.at[1 + h])
        send(wr.at[0, h], w.at[q, pl.ds(h * wh, wh)], ws.at[o], wrecv.at[o], dev_b)
        o = o + HALF_CHUNKS
        arrived(wr.at[1, h], wrecv.at[1 + HALF_CHUNKS + h])
        send(wr.at[1, h], w.at[q2, pl.ds(wb // 2 + h * wh, wh)], ws.at[o], wrecv.at[o], dev_a)

    zs = list(range(2 * n))
    for j in zs[: n // 2 + 2]:
        take_z(j)
    rest = zs[n // 2 + 2:]
    for t in range(half):
        take_d(t)
        take_d(t + half)
        if rest:
            take_z(rest.pop(0))
    for h in range(HALF_CHUNKS):
        for _ in range(len(rest) // (HALF_CHUNKS - h + 1)):
            take_z(rest.pop(0))
        relay_w(h)
    for j in rest:
        take_z(j)

    get_v.wait()
    get_a.wait()
    arrived(v.at[qs, pl.ds(here, nb)], br.at[0, 0])
    for c in range(n):
        arrived(piece(qs, near, c), br.at[1, c])
        arrived(piece(qs2, near, c), br.at[2, c])
        arrived(piece(qs2, here, c), br.at[3, c])
        arrived(piece(qs, far, c), br.at[4, c])
        arrived(piece(qs2, far, c), br.at[5, c])

    first = nb * r - nb

    def image_row(i, carry):
        ix = [jnp.clip(cols_ref[i, s] - first, 0, 3 * nb - 1) for s in range(slots)]
        lhs = jnp.concatenate([a[i, s] for s in range(slots)], axis=1)
        rhs = jnp.concatenate(
            [jnp.concatenate([v[c, at] for c in range(4)], axis=1) for at in ix], axis=0
        )
        total = jnp.dot(lhs, rhs, preferred_element_type=jnp.float32)
        upper = total.astype(jnp.bfloat16)
        hi[i] = upper
        lo[i] = (total - upper.astype(jnp.float32)).astype(jnp.bfloat16)
        return carry

    lax.fori_loop(0, nb, image_row, 0)

    for h in range(HALF_CHUNKS):
        for part in range(2):
            o = 1 + (2 + part) * HALF_CHUNKS + h
            ref = w.at[q2, pl.ds(part * (wb // 2) + h * wh, wh)]
            arrived(ref, wrecv.at[o])
            p = o + 2 * HALF_CHUNKS
            send(ref, ref, ws.at[p], wrecv.at[p], dev_s)
    get_w.wait()
    arrived(w.at[qs], wrecv.at[0])

    dims = (((0,), (0,)), ((), ()))

    def project(slab):
        rows = wb * w.shape[2]
        wv = w[slab].reshape(rows, basis)
        upper = hi[pl.ds(slab * wb, wb)].reshape(rows, basis)
        lower = lo[pl.ds(slab * wb, wb)].reshape(rows, basis)
        out = lax.dot_general(wv, upper, dims, preferred_element_type=jnp.float32)
        out += lax.dot_general(wv, lower, dims, preferred_element_type=jnp.float32)
        return out.reshape(acc.shape)

    acc[...] = project(q)
    acc[...] += project(qs)
    acc[...] += project(q2)
    for h in range(HALF_CHUNKS):
        for part in range(2):
            p = 1 + (4 + part) * HALF_CHUNKS + h
            arrived(w.at[qs2, pl.ds(part * (wb // 2) + h * wh, wh)], wrecv.at[p])
    acc[...] += project(qs2)

    mine = pl.multiple_of(core * (2 * quarter), 2 * quarter)
    theirs = pl.multiple_of((1 - core) * (2 * quarter), 2 * quarter)
    send(acc.at[:, :, :, pl.ds(theirs, 2 * quarter)], r0, qs_sem.at[0], qr_sem.at[0], dev_s)
    arrived(r0, qr_sem.at[0])
    t1[...] = acc[:, :, :, pl.ds(mine, quarter)] + r0[:, :, :, :quarter]
    t2[...] = acc[:, :, :, pl.ds(mine + quarter, quarter)] + r0[:, :, :, quarter:]

    xi = par * 2 + xh
    xis = [(1 - par) * 2 + xh, (1 - par) * 2 + (1 - xh), par * 2 + (1 - xh)]
    row = [dev_a, dev_b, dev_d]

    for e in range(3):
        send(t1.at[:, xis[e]], rx.at[e], qs_sem.at[1 + e], qr_sem.at[1 + e], row[e])
    for j in range(1, pairs):
        copy = pltpu.make_async_remote_copy(
            src_ref=t2.at[(k + j) % pairs], dst_ref=ry.at[j - 1],
            send_sem=qs_sem.at[4], recv_sem=qr_sem.at[4],
            device_id=others[j - 1], device_id_type=MESH,
        )
        copy.start()
    arrived(ry, qr_sem.at[4])
    u2[...] = t2[k] + sum(ry[j] for j in range(pairs - 1))
    for e in range(3):
        send(u2.at[xis[e]], r2x.at[e], qs_sem.at[5 + e], qr_sem.at[5 + e], row[e])
    for e in range(3):
        arrived(rx.at[e], qr_sem.at[1 + e])
    u1[...] = t1[:, xi] + (rx[0] + rx[1] + rx[2])
    for j in range(1, pairs):
        copy = pltpu.make_async_remote_copy(
            src_ref=u1.at[(k + j) % pairs], dst_ref=r2y.at[j - 1],
            send_sem=qs_sem.at[8], recv_sem=qr_sem.at[8],
            device_id=others[j - 1], device_id_type=MESH,
        )
        copy.start()
    for e in range(3):
        arrived(r2x.at[e], qr_sem.at[5 + e])
    second = u2[xi] + (r2x[0] + r2x[1] + r2x[2])
    arrived(r2y, qr_sem.at[8])
    fin[:, :quarter] = u1[k] + sum(r2y[j] for j in range(pairs - 1))
    fin[:, quarter:] = second
    send(fin, rf, qs_sem.at[9], qr_sem.at[9], dev_s)
    arrived(rf, qr_sem.at[9])
    own, other = fin[...], rf[...]
    left = jnp.where(core == 0, own, other)
    right = jnp.where(core == 0, other, own)
    rows = o_ref.shape[0]
    full = jnp.concatenate([left, right], axis=1)
    o_ref[...] = jnp.where(core == 0, full[:rows], full[rows:])

    pltpu.make_async_copy(ry, ry, qs_sem.at[4]).wait()
    pltpu.make_async_copy(r2y, r2y, qs_sem.at[8]).wait()
    for copy in sent:
        copy.wait_send()


def shards(regions, basis_v, basis_w, couplings, coupling_cols):
    nb, slots, block, _ = couplings.shape
    basis = basis_w.shape[1]
    wb = nb // 4
    wh = wb // (2 * HALF_CHUNKS)
    pairs = regions // 2
    group = basis // (4 * pairs)
    quarter = basis // 4
    bf16, f32 = jnp.bfloat16, jnp.float32
    dma = pltpu.SemaphoreType.DMA
    whole = pl.BlockSpec(memory_space=pl.ANY)
    return pl.pallas_call(
        functools.partial(kernel, regions),
        out_shape=jax.ShapeDtypeStruct((group // 2, basis), f32),
        in_specs=[pl.BlockSpec(memory_space=pltpu.SMEM), whole, whole, whole],
        out_specs=pl.BlockSpec(memory_space=pltpu.VMEM),
        scratch_shapes=[
            pltpu.VMEM((nb, slots, block, block), bf16),
            pltpu.VMEM((4, 3 * nb, block, quarter), bf16),
            pltpu.VMEM((4, wb, block, basis), bf16),
            pltpu.VMEM((2, HALF_CHUNKS, wh, block, basis), bf16),
            pltpu.VMEM((nb, block, basis), bf16),
            pltpu.VMEM((nb, block, basis), bf16),
            pltpu.VMEM((pairs, 4, group, basis), f32),
            pltpu.VMEM((pairs, 4, group, 2 * quarter), f32),
            pltpu.VMEM((pairs, 4, group, quarter), f32),
            pltpu.VMEM((pairs, 4, group, quarter), f32),
            pltpu.VMEM((3, pairs, group, quarter), f32),
            pltpu.VMEM((pairs - 1, 4, group, quarter), f32),
            pltpu.VMEM((pairs, group, quarter), f32),
            pltpu.VMEM((4, group, quarter), f32),
            pltpu.VMEM((3, group, quarter), f32),
            pltpu.VMEM((pairs - 1, group, quarter), f32),
            pltpu.VMEM((group, 2 * quarter), f32),
            pltpu.VMEM((group, 2 * quarter), f32),
            dma((3,)),
            dma((5, CHUNKS)), dma((5, CHUNKS)),
            dma((6, CHUNKS)), dma((6, CHUNKS)),
            dma((1 + 6 * HALF_CHUNKS,)), dma((1 + 6 * HALF_CHUNKS,)),
            dma((10,)), dma((10,)),
        ],
        compiler_params=pltpu.CompilerParams(
            collective_id=0, has_side_effects=True, vmem_limit_bytes=67043328
        ),
        name="project",
    )(
        coupling_cols,
        couplings,
        basis_v.reshape(nb, block, quarter),
        basis_w.reshape(wb, block, basis),
    )


def solution(mesh):
    in_specs = (
        P("region", "col"),
        P(("region", "col"), None),
        P("region", "col", None, None),
        P("region", "col"),
    )
    out_specs = P(("region", "col"), None)
    body = functools.partial(shards, mesh.shape["region"])
    return jax.shard_map(body, mesh=mesh, in_specs=in_specs, out_specs=out_specs, check_vma=False)
```

time: 763 us -> 130 us (0.17)
  waiting for transfers between devices: 579 us -> 0 us
  Pallas kernels: 0 us -> 127 us
  local copies, waits for them, and re-layouts: 82 us -> 2.67 us
  matrix products: 57.1 us -> 0 us
  other arithmetic: 24.3 us -> 0 us
  between operations: 13.2 us -> 0.01 us
    ppermute x2 -> x0, waiting for transfers between devices: 268 us -> none  [the longest x1 138 us: extended(): lax.ppermute(lax.slice_in_dim(block, 0, width, axis=dim), axis, backward)]
    unnamed x4 -> x0, waiting for transfers between devices: 149 us -> none
    pallas_call x0 -> x1, Pallas kernels: none -> 127 us  [shards(): pl.pallas_call(functools.partial(kernel, regions), out_shape=jax.ShapeDty...]
    reduce_scatter x1 -> x0, waiting for transfers between devices: 106 us -> none  [shards(): lax.psum_scatter(image_rows(jnp.int32(0), rows_dev // lax.axis_size('col'...]
    gather x6 -> x0, local copies, waits for them, and re-layouts: 79.6 us -> none  [one_group(): picked = widened_blocks[columns]]
    dot_general x8 -> x0, matrix products: 57.1 us -> none  [the longest x6 52.1 us: one_group(): jnp.einsum('gkrs,gksc->grc', blocks, picked, preferred_element_type=jnp.f...]
    all_gather x1 -> x0, waiting for transfers between devices: 56.5 us -> none  [shards(): all_columns = lax.all_gather(basis_v, 'col', axis=1, tiled=True)]
    concatenate x1 -> x0, other arithmetic: 21.4 us -> none  [extended(): block = jnp.concatenate([low, block, high], axis=dim)]
  transfers between devices with their start and end apart: 5 -> 0, of which waited for: 5 -> 0; matrix products, arithmetic and copies ran while one was open for 0% -> 0% of each run, Pallas kernels for 0% -> 0%
where the time goes in v1:
time: 130 us
  Pallas kernels  127 us (98%)
  local copies, waits for them, and re-layouts  2.67 us (2%)
    pallas_call x1, Pallas kernels, shards(): pl.pallas_call(functools.partial(kernel, regions), out_shape=jax.ShapeDty...  127 us
    unnamed x2, local copies, waits for them, and re-layouts  2.67 us

profile of v1, /device:TPU:1, one launch (start us, length us, event | category | flops | bytes accessed | tf_op | source)
XLA Modules:
  0.0 129.8 jit_solution(10758593144381385960)
XLA Ops:
  0.0 1.4 %copy.5.cols_ref = s32[48,12]{1,0:T(8,128)} copy(s32[48,12]{0,1:T(8,128)} %param.7) | data formatting | bytes 4608 | tf_op args[3]
  1.4 127.1 %project.1 = f32[4,512]{1,0:T(4,128)} custom-call(s32[48,12]{1,0:T(8,128)} %copy.5.cols_ref, bf16[48,12,128,128]{3,2,1,0:T(8,128)(2,1)} %a_hbm.1, bf16[48,128,128]{2,1,0:T(8,128)(2,1)} %bitcast.2, bf16[12,128,512]{2,1,0:T(8,128)(2,1)} %bitcast.3), custom_call_target="tpu_custom_call" | custom-call | tf_op jit(solution)/shard_map/project/pallas_call | solution.py:272
  128.5 1.3 copy.7

commit v2 on v1

--- a/solution.py
+++ b/solution.py
@@ -9,12 +9,13 @@
 
 MESH = pl.DeviceIdType.MESH
 CHUNKS = 8
-HALF_CHUNKS = 2
+EARLY, MIDDLE = 5, 2
+HALF_CHUNKS = 3
 
 
 def kernel(
     regions, cols_ref, a_hbm, v_hbm, w_hbm, o_ref,
-    a, v, w, wr, hi, lo, acc, r0, t1, t2, rx, ry, u1, u2, r2x, r2y, fin, rf,
+    a, v, y1, y2, w, wr, hi, lo, acc, r0, t1, t2, rx, ry, u1, u2, r2x, r2y, fin, rf,
     loc, vs, vr, bs, br, ws, wrecv, qs_sem, qr_sem,
 ):
     nb, slots = a.shape[0], a.shape[1]
@@ -39,12 +40,17 @@
     dev_s = (r, qs)
     dev_z = ((r + 2 - 4 * par + regions) % regions, q)
     others = [(((k + j) % pairs) * 2 + par, q) for j in range(1, pairs)]
-    here = nb
-    near = 2 * nb * (1 - par)
-    far = 2 * nb * par
+    ahead = EARLY * (nb // CHUNKS)
+
+    def here(odd):
+        return odd * nb + (1 - odd) * ahead
+
+    def near(odd):
+        return (1 - odd) * (nb + ahead)
+
 
     get_a = pltpu.make_async_copy(a_hbm, a, loc.at[0])
-    get_v = pltpu.make_async_copy(v_hbm, v.at[q, pl.ds(here, nb)], loc.at[1])
+    get_v = pltpu.make_async_copy(v_hbm, v.at[q, pl.ds(here(par), nb)], loc.at[1])
     get_w = pltpu.make_async_copy(w_hbm, w.at[q], loc.at[2])
     get_v.start()
     get_w.start()
@@ -68,55 +74,62 @@
     def arrived(dst, rsem):
         pltpu.make_async_copy(dst, dst, rsem).wait()
 
-    def piece(col, base, c):
-        return v.at[col, pl.ds(base + c * cb, cb)]
-
-    for t in range(n):
-        c = t
-        send(v_hbm.at[pl.ds(c * cb, cb)], piece(q, far, c), vs.at[0, c], vr.at[0, c], dev_a)
-        c = (t + half) % n
-        send(v_hbm.at[pl.ds(c * cb, cb)], piece(q, far, c), vs.at[1, c], vr.at[1, c], dev_b)
-    send(v_hbm, v.at[q, pl.ds(here, nb)], bs.at[0, 0], br.at[0, 0], dev_s)
+    def place(odd, c):
+        return odd * (n - 1 - c) * cb + (1 - odd) * c * cb
+
+    def piece_here(col, odd, c):
+        return v.at[col, pl.ds(here(odd) + place(odd, c), cb)]
+
+    def piece_near(col, odd, c):
+        return v.at[col, pl.ds(near(odd) + place(1 - odd, c), cb)]
+
+    def piece_far(col, c):
+        if c < EARLY:
+            return v.at[col, pl.ds(par * (2 * nb + c * cb) + (1 - par) * (EARLY - 1 - c) * cb, cb)]
+        if c < EARLY + MIDDLE:
+            e = c - EARLY
+            return y1.at[col, pl.ds(par * e * cb + (1 - par) * (MIDDLE - 1 - e) * cb, cb)]
+        e, late = c - EARLY - MIDDLE, n - EARLY - MIDDLE
+        return y2.at[col, pl.ds(par * e * cb + (1 - par) * (late - 1 - e) * cb, cb)]
+
+    for c in range(n):
+        src = v_hbm.at[pl.ds(place(par, c), cb)]
+        send(src, piece_near(q, 1 - par, c), vs.at[0, c], vr.at[0, c], dev_a)
+        send(src, piece_near(q, 1 - par, c), vs.at[1, c], vr.at[1, c], dev_b)
+    send(v_hbm, v.at[q, pl.ds(here(par), nb)], bs.at[0, 0], br.at[0, 0], dev_s)
     send(w_hbm, w.at[q], ws.at[0], wrecv.at[0], dev_s)
     get_a.start()
 
-    def to_sibling(slab, col, base, c):
-        ref = piece(col, base, c)
+    def to_sibling(slab, ref, c):
         send(ref, ref, bs.at[slab, c], br.at[slab, c], dev_s)
 
-    def take_a(c):
-        arrived(piece(q, near, c), vr.at[0, c])
-        src = piece(q, near, c)
-        send(src, piece(q, far, c), vs.at[3, c], vr.at[3, c], dev_z)
+    def take_near(c):
+        ref = piece_near(q, par, c)
+        arrived(ref, vr.at[0, c])
+        send(ref, piece_far(q, c), vs.at[3, c], vr.at[3, c], dev_z)
         if c < half:
-            send(src, piece(q, here, c), vs.at[2, c], vr.at[2, c], dev_b)
-        to_sibling(1, q, near, c)
-
-    def take_b(c):
-        arrived(piece(q2, near, c), vr.at[1, c])
-        src = piece(q2, near, c)
-        send(src, piece(q2, far, c), vs.at[4, c], vr.at[4, c], dev_z)
+            send(ref, piece_here(q, 1 - par, c), vs.at[2, c], vr.at[2, c], dev_b)
+        to_sibling(1, ref, c)
+        ref = piece_near(q2, par, c)
+        arrived(ref, vr.at[1, c])
+        send(ref, piece_far(q2, c), vs.at[4, c], vr.at[4, c], dev_z)
         if c >= half:
-            send(src, piece(q2, here, c), vs.at[2, c], vr.at[2, c], dev_a)
-        to_sibling(2, q2, near, c)
-
-    def take_d(c):
-        arrived(piece(q2, here, c), vr.at[2, c])
-        to_sibling(3, q2, here, c)
-
-    def take_z(j):
-        c = j // 2
-        if j % 2 == 0:
-            arrived(piece(q, far, c), vr.at[3, c])
-            to_sibling(4, q, far, c)
-        else:
-            c = (c + half) % n
-            arrived(piece(q2, far, c), vr.at[4, c])
-            to_sibling(5, q2, far, c)
-
-    for t in range(n):
-        take_a(t)
-        take_b((t + half) % n)
+            send(ref, piece_here(q2, 1 - par, c), vs.at[2, c], vr.at[2, c], dev_a)
+        to_sibling(2, ref, c)
+
+    def take_here(c):
+        ref = piece_here(q2, par, c)
+        arrived(ref, vr.at[2, c])
+        to_sibling(3, ref, c)
+
+    def take_far(c):
+        for e, col in ((3, q), (4, q2)):
+            ref = piece_far(col, c)
+            arrived(ref, vr.at[e, c])
+            to_sibling(e + 1, ref, c)
+
+    for c in range(n):
+        take_near(c)
 
     for h in range(HALF_CHUNKS):
         send(w_hbm.at[pl.ds(h * wh, wh)], wr.at[0, h], ws.at[1 + h], wrecv.at[1 + h], dev_a)
@@ -131,48 +144,96 @@
         arrived(wr.at[1, h], wrecv.at[1 + HALF_CHUNKS + h])
         send(wr.at[1, h], w.at[q2, pl.ds(wb // 2 + h * wh, wh)], ws.at[o], wrecv.at[o], dev_a)
 
-    zs = list(range(2 * n))
-    for j in zs[: n // 2 + 2]:
-        take_z(j)
-    rest = zs[n // 2 + 2:]
-    for t in range(half):
-        take_d(t)
-        take_d(t + half)
-        if rest:
-            take_z(rest.pop(0))
-    for h in range(HALF_CHUNKS):
-        for _ in range(len(rest) // (HALF_CHUNKS - h + 1)):
-            take_z(rest.pop(0))
-        relay_w(h)
-    for j in rest:
-        take_z(j)
+    for c in range(half - 1):
+        take_far(c)
+    for c in range(half):
+        take_here(c)
+        take_here(c + half)
+        if c >= half - 2:
+            take_far(half - 1 + c - (half - 2))
 
     get_v.wait()
     get_a.wait()
-    arrived(v.at[qs, pl.ds(here, nb)], br.at[0, 0])
+    arrived(v.at[qs, pl.ds(here(par), nb)], br.at[0, 0])
     for c in range(n):
-        arrived(piece(qs, near, c), br.at[1, c])
-        arrived(piece(qs2, near, c), br.at[2, c])
-        arrived(piece(qs2, here, c), br.at[3, c])
-        arrived(piece(qs, far, c), br.at[4, c])
-        arrived(piece(qs2, far, c), br.at[5, c])
-
-    first = nb * r - nb
-
-    def image_row(i, carry):
-        ix = [jnp.clip(cols_ref[i, s] - first, 0, 3 * nb - 1) for s in range(slots)]
-        lhs = jnp.concatenate([a[i, s] for s in range(slots)], axis=1)
-        rhs = jnp.concatenate(
-            [jnp.concatenate([v[c, at] for c in range(4)], axis=1) for at in ix], axis=0
-        )
-        total = jnp.dot(lhs, rhs, preferred_element_type=jnp.float32)
-        upper = total.astype(jnp.bfloat16)
-        hi[i] = upper
-        lo[i] = (total - upper.astype(jnp.float32)).astype(jnp.bfloat16)
-        return carry
-
-    lax.fori_loop(0, nb, image_row, 0)
-
+        arrived(piece_near(qs, par, c), br.at[1, c])
+        arrived(piece_near(qs2, par, c), br.at[2, c])
+        arrived(piece_here(qs2, par, c), br.at[3, c])
+
+    def image_rows(c):
+        start = place(1 - par, c)
+        held = [v] + ([y1] if c >= EARLY else []) + ([y2] if c >= EARLY + MIDDLE else [])
+        away = nb * (r - 1 + 2 * par)
+        bases = [
+            nb * r - par * nb - (1 - par) * ahead,
+            away + par * ahead + (1 - par) * (n - EARLY - MIDDLE) * cb,
+            away + par * (EARLY + MIDDLE) * cb,
+        ]
+
+        def chosen(col, at):
+            out = held[0][col, jnp.clip(at - bases[0], 0, held[0].shape[1] - 1)]
+            for e in range(1, len(held)):
+                inside = (at >= bases[e]) & (at < bases[e] + held[e].shape[1])
+                other = held[e][col, jnp.clip(at - bases[e], 0, held[e].shape[1] - 1)]
+                out = jnp.where(inside, other, out)
+            return out
+
+        def image_row(t, carry):
+            i = start + t
+            lhs = jnp.concatenate([a[i, s] for s in range(slots)], axis=1)
+            rhs = jnp.concatenate(
+                [
+                    jnp.concatenate([chosen(col, cols_ref[s, i]) for col in range(4)], axis=1)
+                    for s in range(slots)
+                ],
+                axis=0,
+            )
+            total = jnp.dot(lhs, rhs, preferred_element_type=jnp.float32)
+            upper = total.astype(jnp.bfloat16)
+            hi[i] = upper
+            lo[i] = (total - upper.astype(jnp.float32)).astype(jnp.bfloat16)
+            return carry
+
+        lax.fori_loop(0, cb, image_row, 0)
+
+    def all_far(first, last):
+        for c in range(first, last):
+            arrived(piece_far(qs, c), br.at[4, c])
+            arrived(piece_far(qs2, c), br.at[5, c])
+
+    all_far(0, EARLY)
+    image_rows(0)
+    take_far(5)
+    image_rows(1)
+    relay_w(0)
+    image_rows(2)
+    image_rows(3)
+    relay_w(1)
+    image_rows(4)
+    take_far(6)
+    all_far(EARLY, EARLY + MIDDLE)
+    image_rows(5)
+    relay_w(2)
+    image_rows(6)
+    take_far(7)
+    all_far(EARLY + MIDDLE, n)
+    image_rows(7)
+
+    dims = (((0,), (0,)), ((), ()))
+
+    def project(slab, at, count):
+        rows = count * w.shape[2]
+        wv = w[slab, at:at + count].reshape(rows, basis)
+        upper = hi[pl.ds(slab * wb + at, count)].reshape(rows, basis)
+        lower = lo[pl.ds(slab * wb + at, count)].reshape(rows, basis)
+        out = lax.dot_general(wv, upper, dims, preferred_element_type=jnp.float32)
+        out += lax.dot_general(wv, lower, dims, preferred_element_type=jnp.float32)
+        return out.reshape(acc.shape)
+
+    get_w.wait()
+    acc[...] = project(q, 0, wb)
+    arrived(w.at[qs], wrecv.at[0])
+    acc[...] += project(qs, 0, wb)
     for h in range(HALF_CHUNKS):
         for part in range(2):
             o = 1 + (2 + part) * HALF_CHUNKS + h
@@ -180,28 +241,12 @@
             arrived(ref, wrecv.at[o])
             p = o + 2 * HALF_CHUNKS
             send(ref, ref, ws.at[p], wrecv.at[p], dev_s)
-    get_w.wait()
-    arrived(w.at[qs], wrecv.at[0])
-
-    dims = (((0,), (0,)), ((), ()))
-
-    def project(slab):
-        rows = wb * w.shape[2]
-        wv = w[slab].reshape(rows, basis)
-        upper = hi[pl.ds(slab * wb, wb)].reshape(rows, basis)
-        lower = lo[pl.ds(slab * wb, wb)].reshape(rows, basis)
-        out = lax.dot_general(wv, upper, dims, preferred_element_type=jnp.float32)
-        out += lax.dot_general(wv, lower, dims, preferred_element_type=jnp.float32)
-        return out.reshape(acc.shape)
-
-    acc[...] = project(q)
-    acc[...] += project(qs)
-    acc[...] += project(q2)
-    for h in range(HALF_CHUNKS):
+        for part in range(2):
+            acc[...] += project(q2, part * (wb // 2) + h * wh, wh)
         for part in range(2):
             p = 1 + (4 + part) * HALF_CHUNKS + h
             arrived(w.at[qs2, pl.ds(part * (wb // 2) + h * wh, wh)], wrecv.at[p])
-    acc[...] += project(qs2)
+            acc[...] += project(qs2, part * (wb // 2) + h * wh, wh)
 
     mine = pl.multiple_of(core * (2 * quarter), 2 * quarter)
     theirs = pl.multiple_of((1 - core) * (2 * quarter), 2 * quarter)
@@ -261,6 +306,7 @@
 def shards(regions, basis_v, basis_w, couplings, coupling_cols):
     nb, slots, block, _ = couplings.shape
     basis = basis_w.shape[1]
+    cb = nb // CHUNKS
     wb = nb // 4
     wh = wb // (2 * HALF_CHUNKS)
     pairs = regions // 2
@@ -276,7 +322,9 @@
         out_specs=pl.BlockSpec(memory_space=pltpu.VMEM),
         scratch_shapes=[
             pltpu.VMEM((nb, slots, block, block), bf16),
-            pltpu.VMEM((4, 3 * nb, block, quarter), bf16),
+            pltpu.VMEM((4, 2 * nb + EARLY * cb, block, quarter), bf16),
+            pltpu.VMEM((4, MIDDLE * cb, block, quarter), bf16),
+            pltpu.VMEM((4, (CHUNKS - EARLY - MIDDLE) * cb, block, quarter), bf16),
             pltpu.VMEM((4, wb, block, basis), bf16),
             pltpu.VMEM((2, HALF_CHUNKS, wh, block, basis), bf16),
             pltpu.VMEM((nb, block, basis), bf16),
@@ -304,7 +352,7 @@
         ),
         name="project",
     )(
-        coupling_cols,
+        coupling_cols.T,
         couplings,
         basis_v.reshape(nb, block, quarter),
         basis_w.reshape(wb, block, basis),

time: 130 us -> 121 us (0.931)
  Pallas kernels: 127 us -> 119 us
  local copies, waits for them, and re-layouts: 2.67 us -> 1.3 us
    pallas_call x1, Pallas kernels: 127 us -> 119 us  [shards(): pl.pallas_call(functools.partial(kernel, regions), out_shape=jax.ShapeDty...]
    unnamed x2 -> x1, local copies, waits for them, and re-layouts: 2.67 us -> 1.3 us
where the time goes in v2:
time: 121 us
  Pallas kernels  119 us (98%)
  local copies, waits for them, and re-layouts  1.3 us (1%)
    pallas_call x1, Pallas kernels, shards(): pl.pallas_call(functools.partial(kernel, regions), out_shape=jax.ShapeDty...  119 us

profile of v2, /device:TPU:1, one launch (start us, length us, event | category | flops | bytes accessed | tf_op | source)
XLA Modules:
  0.0 120.8 jit_solution(6136296984112070001)
XLA Ops:
  0.0 119.5 %project.1 = f32[4,512]{1,0:T(4,128)} custom-call(s32[12,48]{1,0:T(8,128)} %bitcast.5, bf16[48,12,128,128]{3,2,1,0:T(8,128)(2,1)} %a_hbm.1, bf16[48,128,128]{2,1,0:T(8,128)(2,1)} %bitcast.3, bf16[12,128,512]{2,1,0:T(8,128)(2,1)} %bitcast.4), custom_call_target="tpu_custom_call" | custom-call | tf_op jit(solution)/shard_map/project/pallas_call | solution.py:318
  119.5 1.3 %copy.6 = f32[4,512]{1,0:T(4,128)} copy(f32[4,512]{1,0:T(4,128)} %project.1) | data formatting | bytes 16384

commit v3 on v2

--- a/solution.py
+++ b/solution.py
@@ -201,6 +201,30 @@
             arrived(piece_far(qs, c), br.at[4, c])
             arrived(piece_far(qs2, c), br.at[5, c])
 
+    dims = (((0,), (0,)), ((), ()))
+
+    def product(pieces):
+        rows = sum(count for _, count, _ in pieces) * w.shape[2]
+        wv = jnp.concatenate([wv for _, _, wv in pieces], axis=0).reshape(rows, basis)
+        upper, lower = [
+            jnp.concatenate([ref[pl.ds(at, count)] for at, count, _ in pieces], axis=0)
+            .reshape(rows, basis)
+            for ref in (hi, lo)
+        ]
+        out = lax.dot_general(wv, upper, dims, preferred_element_type=jnp.float32)
+        out += lax.dot_general(wv, lower, dims, preferred_element_type=jnp.float32)
+        return out.reshape(acc.shape)
+
+    late = par * xh + (1 - par) * (1 - xh)
+
+    def own_rows(m):
+        at = (1 - par) * (n - 1 - m - late * half) * cb + par * (m + late * half) * cb
+        slab = at // wb
+        return at, cb, w[slab, pl.ds(at - slab * wb, cb)]
+
+    def own_part(groups):
+        return product([own_rows(m) for m in groups])
+
     all_far(0, EARLY)
     image_rows(0)
     take_far(5)
@@ -215,25 +239,18 @@
     image_rows(5)
     relay_w(2)
     image_rows(6)
+    get_w.wait()
+    arrived(w.at[qs], wrecv.at[0])
+    acc[...] = own_part([0, 1, 2])
     take_far(7)
     all_far(EARLY + MIDDLE, n)
     image_rows(7)
-
-    dims = (((0,), (0,)), ((), ()))
-
-    def project(slab, at, count):
-        rows = count * w.shape[2]
-        wv = w[slab, at:at + count].reshape(rows, basis)
-        upper = hi[pl.ds(slab * wb + at, count)].reshape(rows, basis)
-        lower = lo[pl.ds(slab * wb + at, count)].reshape(rows, basis)
-        out = lax.dot_general(wv, upper, dims, preferred_element_type=jnp.float32)
-        out += lax.dot_general(wv, lower, dims, preferred_element_type=jnp.float32)
-        return out.reshape(acc.shape)
-
-    get_w.wait()
-    acc[...] = project(q, 0, wb)
-    arrived(w.at[qs], wrecv.at[0])
-    acc[...] += project(qs, 0, wb)
+    acc[...] += own_part([3])
+
+    def both(slab, h):
+        ats = [part * (wb // 2) + h * wh for part in range(2)]
+        return product([(slab * wb + at, wh, w[slab, at:at + wh]) for at in ats])
+
     for h in range(HALF_CHUNKS):
         for part in range(2):
             o = 1 + (2 + part) * HALF_CHUNKS + h
@@ -241,55 +258,52 @@
             arrived(ref, wrecv.at[o])
             p = o + 2 * HALF_CHUNKS
             send(ref, ref, ws.at[p], wrecv.at[p], dev_s)
-        for part in range(2):
-            acc[...] += project(q2, part * (wb // 2) + h * wh, wh)
+        acc[...] += both(q2, h)
         for part in range(2):
             p = 1 + (4 + part) * HALF_CHUNKS + h
             arrived(w.at[qs2, pl.ds(part * (wb // 2) + h * wh, wh)], wrecv.at[p])
-            acc[...] += project(qs2, part * (wb // 2) + h * wh, wh)
+        acc[...] += both(qs2, h)
 
     mine = pl.multiple_of(core * (2 * quarter), 2 * quarter)
     theirs = pl.multiple_of((1 - core) * (2 * quarter), 2 * quarter)
-    send(acc.at[:, :, :, pl.ds(theirs, 2 * quarter)], r0, qs_sem.at[0], qr_sem.at[0], dev_s)
-    arrived(r0, qr_sem.at[0])
-    t1[...] = acc[:, :, :, pl.ds(mine, quarter)] + r0[:, :, :, :quarter]
-    t2[...] = acc[:, :, :, pl.ds(mine + quarter, quarter)] + r0[:, :, :, quarter:]
+    for e in (1, 0):
+        cut = acc.at[:, :, :, pl.ds(theirs + e * quarter, quarter)]
+        send(cut, r0.at[e], qs_sem.at[e], qr_sem.at[e], dev_s)
+
+    def scatter(src, dst, ssem, rsem):
+        for j in range(1, pairs):
+            pltpu.make_async_remote_copy(
+                src_ref=src.at[(k + j) % pairs], dst_ref=dst.at[j - 1],
+                send_sem=ssem, recv_sem=rsem,
+                device_id=others[j - 1], device_id_type=MESH,
+            ).start()
 
     xi = par * 2 + xh
     xis = [(1 - par) * 2 + xh, (1 - par) * 2 + (1 - xh), par * 2 + (1 - xh)]
     row = [dev_a, dev_b, dev_d]
-
+    arrived(r0.at[1], qr_sem.at[1])
+    t2[...] = acc[:, :, :, pl.ds(mine + quarter, quarter)] + r0[1]
+    scatter(t2, ry, qs_sem.at[5], qr_sem.at[5])
+    arrived(r0.at[0], qr_sem.at[0])
+    t1[...] = acc[:, :, :, pl.ds(mine, quarter)] + r0[0]
     for e in range(3):
-        send(t1.at[:, xis[e]], rx.at[e], qs_sem.at[1 + e], qr_sem.at[1 + e], row[e])
-    for j in range(1, pairs):
-        copy = pltpu.make_async_remote_copy(
-            src_ref=t2.at[(k + j) % pairs], dst_ref=ry.at[j - 1],
-            send_sem=qs_sem.at[4], recv_sem=qr_sem.at[4],
-            device_id=others[j - 1], device_id_type=MESH,
-        )
-        copy.start()
-    arrived(ry, qr_sem.at[4])
+        send(t1.at[:, xis[e]], rx.at[e], qs_sem.at[2 + e], qr_sem.at[2 + e], row[e])
+    for e in range(3):
+        arrived(rx.at[e], qr_sem.at[2 + e])
+    u1[...] = t1[:, xi] + (rx[0] + rx[1] + rx[2])
+    scatter(u1, r2y, qs_sem.at[9], qr_sem.at[9])
+    arrived(ry, qr_sem.at[5])
     u2[...] = t2[k] + sum(ry[j] for j in range(pairs - 1))
     for e in range(3):
-        send(u2.at[xis[e]], r2x.at[e], qs_sem.at[5 + e], qr_sem.at[5 + e], row[e])
+        send(u2.at[xis[e]], r2x.at[e], qs_sem.at[6 + e], qr_sem.at[6 + e], row[e])
     for e in range(3):
-        arrived(rx.at[e], qr_sem.at[1 + e])
-    u1[...] = t1[:, xi] + (rx[0] + rx[1] + rx[2])
-    for j in range(1, pairs):
-        copy = pltpu.make_async_remote_copy(
-            src_ref=u1.at[(k + j) % pairs], dst_ref=r2y.at[j - 1],
-            send_sem=qs_sem.at[8], recv_sem=qr_sem.at[8],
-            device_id=others[j - 1], device_id_type=MESH,
-        )
-        copy.start()
-    for e in range(3):
-        arrived(r2x.at[e], qr_sem.at[5 + e])
+        arrived(r2x.at[e], qr_sem.at[6 + e])
     second = u2[xi] + (r2x[0] + r2x[1] + r2x[2])
-    arrived(r2y, qr_sem.at[8])
+    arrived(r2y, qr_sem.at[9])
     fin[:, :quarter] = u1[k] + sum(r2y[j] for j in range(pairs - 1))
     fin[:, quarter:] = second
-    send(fin, rf, qs_sem.at[9], qr_sem.at[9], dev_s)
-    arrived(rf, qr_sem.at[9])
+    send(fin, rf, qs_sem.at[10], qr_sem.at[10], dev_s)
+    arrived(rf, qr_sem.at[10])
     own, other = fin[...], rf[...]
     left = jnp.where(core == 0, own, other)
     right = jnp.where(core == 0, other, own)
@@ -297,8 +311,8 @@
     full = jnp.concatenate([left, right], axis=1)
     o_ref[...] = jnp.where(core == 0, full[:rows], full[rows:])
 
-    pltpu.make_async_copy(ry, ry, qs_sem.at[4]).wait()
-    pltpu.make_async_copy(r2y, r2y, qs_sem.at[8]).wait()
+    arrived(ry, qs_sem.at[5])
+    arrived(r2y, qs_sem.at[9])
     for copy in sent:
         copy.wait_send()
 
@@ -330,7 +344,7 @@
             pltpu.VMEM((nb, block, basis), bf16),
             pltpu.VMEM((nb, block, basis), bf16),
             pltpu.VMEM((pairs, 4, group, basis), f32),
-            pltpu.VMEM((pairs, 4, group, 2 * quarter), f32),
+            pltpu.VMEM((2, pairs, 4, group, quarter), f32),
             pltpu.VMEM((pairs, 4, group, quarter), f32),
             pltpu.VMEM((pairs, 4, group, quarter), f32),
             pltpu.VMEM((3, pairs, group, quarter), f32),
@@ -345,7 +359,7 @@
             dma((5, CHUNKS)), dma((5, CHUNKS)),
             dma((6, CHUNKS)), dma((6, CHUNKS)),
             dma((1 + 6 * HALF_CHUNKS,)), dma((1 + 6 * HALF_CHUNKS,)),
-            dma((10,)), dma((10,)),
+            dma((11,)), dma((11,)),
         ],
         compiler_params=pltpu.CompilerParams(
             collective_id=0, has_side_effects=True, vmem_limit_bytes=67043328

time: 121 us -> 120 us (level)
  no operation moved by 1% of the time
where the time goes in v3:
time: 120 us
  Pallas kernels  119 us (99%)
  local copies, waits for them, and re-layouts  1.3 us (1%)
    pallas_call x1, Pallas kernels, shards(): pl.pallas_call(functools.partial(kernel, regions), out_shape=jax.ShapeDty...  119 us

profile of v3, /device:TPU:1, one launch (start us, length us, event | category | flops | bytes accessed | tf_op | source)
XLA Modules:
  0.0 120.3 jit_solution(16144074961465627278)
XLA Ops:
  0.0 119.0 %project.1 = f32[4,512]{1,0:T(4,128)} custom-call(s32[12,48]{1,0:T(8,128)} %bitcast.5, bf16[48,12,128,128]{3,2,1,0:T(8,128)(2,1)} %a_hbm.1, bf16[48,128,128]{2,1,0:T(8,128)(2,1)} %bitcast.3, bf16[12,128,512]{2,1,0:T(8,128)(2,1)} %bitcast.4), custom_call_target="tpu_custom_call" | custom-call | tf_op jit(solution)/shard_map/project/pallas_call | solution.py:332
  119.0 1.3 %copy.6 = f32[4,512]{1,0:T(4,128)} copy(f32[4,512]{1,0:T(4,128)} %project.1) | data formatting | bytes 16384

commit v4 on v3

--- a/solution.py
+++ b/solution.py
@@ -15,8 +15,8 @@
 
 def kernel(
     regions, cols_ref, a_hbm, v_hbm, w_hbm, o_ref,
-    a, v, y1, y2, w, wr, hi, lo, acc, r0, t1, t2, rx, ry, u1, u2, r2x, r2y, fin, rf,
-    loc, vs, vr, bs, br, ws, wrecv, qs_sem, qr_sem,
+    a, v, y1, y2, w, wr, acc, r0, t1, t2, rx, ry, u1, u2, r2x, r2y, fin, rf,
+    xs, loc, vs, vr, bs, br, ws, wrecv, xsend, xrecv, qs_sem, qr_sem,
 ):
     nb, slots = a.shape[0], a.shape[1]
     n, half = CHUNKS, CHUNKS // 2
@@ -40,17 +40,11 @@
     dev_s = (r, qs)
     dev_z = ((r + 2 - 4 * par + regions) % regions, q)
     others = [(((k + j) % pairs) * 2 + par, q) for j in range(1, pairs)]
-    ahead = EARLY * (nb // CHUNKS)
-
-    def here(odd):
-        return odd * nb + (1 - odd) * ahead
-
     def near(odd):
-        return (1 - odd) * (nb + ahead)
-
+        return 2 * nb * (1 - odd)
 
     get_a = pltpu.make_async_copy(a_hbm, a, loc.at[0])
-    get_v = pltpu.make_async_copy(v_hbm, v.at[q, pl.ds(here(par), nb)], loc.at[1])
+    get_v = pltpu.make_async_copy(v_hbm, v.at[q, pl.ds(nb, nb)], loc.at[1])
     get_w = pltpu.make_async_copy(w_hbm, w.at[q], loc.at[2])
     get_v.start()
     get_w.start()
@@ -78,14 +72,14 @@
         return odd * (n - 1 - c) * cb + (1 - odd) * c * cb
 
     def piece_here(col, odd, c):
-        return v.at[col, pl.ds(here(odd) + place(odd, c), cb)]
+        return v.at[col, pl.ds(nb + place(odd, c), cb)]
 
     def piece_near(col, odd, c):
         return v.at[col, pl.ds(near(odd) + place(1 - odd, c), cb)]
 
     def piece_far(col, c):
         if c < EARLY:
-            return v.at[col, pl.ds(par * (2 * nb + c * cb) + (1 - par) * (EARLY - 1 - c) * cb, cb)]
+            return v.at[col, pl.ds(par * 2 * nb + place(1 - par, c), cb)]
         if c < EARLY + MIDDLE:
             e = c - EARLY
             return y1.at[col, pl.ds(par * e * cb + (1 - par) * (MIDDLE - 1 - e) * cb, cb)]
@@ -96,7 +90,7 @@
         src = v_hbm.at[pl.ds(place(par, c), cb)]
         send(src, piece_near(q, 1 - par, c), vs.at[0, c], vr.at[0, c], dev_a)
         send(src, piece_near(q, 1 - par, c), vs.at[1, c], vr.at[1, c], dev_b)
-    send(v_hbm, v.at[q, pl.ds(here(par), nb)], bs.at[0, 0], br.at[0, 0], dev_s)
+    send(v_hbm, v.at[q, pl.ds(nb, nb)], bs.at[0, 0], br.at[0, 0], dev_s)
     send(w_hbm, w.at[q], ws.at[0], wrecv.at[0], dev_s)
     get_a.start()
 
@@ -154,7 +148,7 @@
 
     get_v.wait()
     get_a.wait()
-    arrived(v.at[qs, pl.ds(here(par), nb)], br.at[0, 0])
+    arrived(v.at[qs, pl.ds(nb, nb)], br.at[0, 0])
     for c in range(n):
         arrived(piece_near(qs, par, c), br.at[1, c])
         arrived(piece_near(qs2, par, c), br.at[2, c])
@@ -162,36 +156,21 @@
 
     def image_rows(c):
         start = place(1 - par, c)
-        held = [v] + ([y1] if c >= EARLY else []) + ([y2] if c >= EARLY + MIDDLE else [])
-        away = nb * (r - 1 + 2 * par)
-        bases = [
-            nb * r - par * nb - (1 - par) * ahead,
-            away + par * ahead + (1 - par) * (n - EARLY - MIDDLE) * cb,
-            away + par * (EARLY + MIDDLE) * cb,
-        ]
-
-        def chosen(col, at):
-            out = held[0][col, jnp.clip(at - bases[0], 0, held[0].shape[1] - 1)]
-            for e in range(1, len(held)):
-                inside = (at >= bases[e]) & (at < bases[e] + held[e].shape[1])
-                other = held[e][col, jnp.clip(at - bases[e], 0, held[e].shape[1] - 1)]
-                out = jnp.where(inside, other, out)
-            return out
+        first = nb * r - nb
 
         def image_row(t, carry):
             i = start + t
+            ix = [jnp.clip(cols_ref[s, i] - first, 0, 3 * nb - 1) for s in range(slots)]
             lhs = jnp.concatenate([a[i, s] for s in range(slots)], axis=1)
             rhs = jnp.concatenate(
-                [
-                    jnp.concatenate([chosen(col, cols_ref[s, i]) for col in range(4)], axis=1)
-                    for s in range(slots)
-                ],
-                axis=0,
+                [jnp.concatenate([v[col, at] for col in range(4)], axis=1) for at in ix], axis=0
             )
             total = jnp.dot(lhs, rhs, preferred_element_type=jnp.float32)
             upper = total.astype(jnp.bfloat16)
-            hi[i] = upper
-            lo[i] = (total - upper.astype(jnp.float32)).astype(jnp.bfloat16)
+            lower = (total - upper.astype(jnp.float32)).astype(jnp.bfloat16)
+            for col in range(4):
+                a[i, col] = upper[:, col * quarter:(col + 1) * quarter]
+                a[i, 4 + col] = lower[:, col * quarter:(col + 1) * quarter]
             return carry
 
         lax.fori_loop(0, cb, image_row, 0)
@@ -203,13 +182,16 @@
 
     dims = (((0,), (0,)), ((), ()))
 
+    def image(at, count, first, cols=4):
+        tiles = [a[pl.ds(at, count), first + e].reshape(count * a.shape[2], quarter) for e in range(cols)]
+        return jnp.concatenate(tiles, axis=1)
+
     def product(pieces):
         rows = sum(count for _, count, _ in pieces) * w.shape[2]
         wv = jnp.concatenate([wv for _, _, wv in pieces], axis=0).reshape(rows, basis)
         upper, lower = [
-            jnp.concatenate([ref[pl.ds(at, count)] for at, count, _ in pieces], axis=0)
-            .reshape(rows, basis)
-            for ref in (hi, lo)
+            jnp.concatenate([image(at, count, e) for at, count, _ in pieces], axis=0)
+            for e in (0, 4)
         ]
         out = lax.dot_general(wv, upper, dims, preferred_element_type=jnp.float32)
         out += lax.dot_general(wv, lower, dims, preferred_element_type=jnp.float32)
@@ -224,6 +206,11 @@
 
     def own_part(groups):
         return product([own_rows(m) for m in groups])
+
+    at1 = par * (2 * nb + EARLY * cb) + (1 - par) * (n - EARLY - MIDDLE) * cb
+    at2 = par * (2 * nb + (EARLY + MIDDLE) * cb)
+    put1 = pltpu.make_async_copy(y1, v.at[:, pl.ds(at1, MIDDLE * cb)], loc.at[3])
+    put2 = pltpu.make_async_copy(y2, v.at[:, pl.ds(at2, (n - EARLY - MIDDLE) * cb)], loc.at[4])
 
     all_far(0, EARLY)
     image_rows(0)
@@ -236,39 +223,102 @@
     image_rows(4)
     take_far(6)
     all_far(EARLY, EARLY + MIDDLE)
+    put1.start()
+    get_w.wait()
+    arrived(w.at[qs], wrecv.at[0])
+    acc[...] = own_part([0])
+    put1.wait()
     image_rows(5)
     relay_w(2)
     image_rows(6)
-    get_w.wait()
-    arrived(w.at[qs], wrecv.at[0])
-    acc[...] = own_part([0, 1, 2])
     take_far(7)
     all_far(EARLY + MIDDLE, n)
+    put2.start()
+    acc[...] += own_part([1, 2])
+    put2.wait()
     image_rows(7)
+
+    mine = pl.multiple_of(core * (2 * quarter), 2 * quarter)
+    theirs = pl.multiple_of((1 - core) * (2 * quarter), 2 * quarter)
+    last = HALF_CHUNKS - 1
+    lasts = [(e, part) for e in range(2) for part in range(2)]
+
+    def last_rows(slab, part):
+        return slab * wb + part * (wb // 2) + last * wh
+
+    for e, part in lasts:
+        at = last_rows(2 * (1 - xh) + e, part)
+        for f in range(2):
+            cut = a.at[pl.ds(at, wh), pl.ds(4 * f + 2 * (1 - core), 2)]
+            g = 4 * e + 2 * part + f
+            send(cut, xs.at[e, part, f], xsend.at[g], xrecv.at[g], dev_s)
     acc[...] += own_part([3])
 
     def both(slab, h):
         ats = [part * (wb // 2) + h * wh for part in range(2)]
         return product([(slab * wb + at, wh, w[slab, at:at + wh]) for at in ats])
 
-    for h in range(HALF_CHUNKS):
+    def w_arrived(h):
         for part in range(2):
             o = 1 + (2 + part) * HALF_CHUNKS + h
             ref = w.at[q2, pl.ds(part * (wb // 2) + h * wh, wh)]
             arrived(ref, wrecv.at[o])
             p = o + 2 * HALF_CHUNKS
             send(ref, ref, ws.at[p], wrecv.at[p], dev_s)
-        acc[...] += both(q2, h)
+
+    def w_forwarded(h):
         for part in range(2):
             p = 1 + (4 + part) * HALF_CHUNKS + h
             arrived(w.at[qs2, pl.ds(part * (wb // 2) + h * wh, wh)], wrecv.at[p])
+
+    for h in range(last):
+        w_arrived(h)
+        acc[...] += both(q2, h)
+        w_forwarded(h)
         acc[...] += both(qs2, h)
 
-    mine = pl.multiple_of(core * (2 * quarter), 2 * quarter)
-    theirs = pl.multiple_of((1 - core) * (2 * quarter), 2 * quarter)
     for e in (1, 0):
         cut = acc.at[:, :, :, pl.ds(theirs + e * quarter, quarter)]
         send(cut, r0.at[e], qs_sem.at[e], qr_sem.at[e], dev_s)
+    for e, part in lasts:
+        for f in range(2):
+            arrived(xs.at[e, part, f], xrecv.at[4 * e + 2 * part + f])
+    arrived(r0.at[1], qr_sem.at[1])
+    t2[...] = acc[:, :, :, pl.ds(mine + quarter, quarter)] + r0[1]
+    arrived(r0.at[0], qr_sem.at[0])
+    t1[...] = acc[:, :, :, pl.ds(mine, quarter)] + r0[0]
+
+    def last_product(slab, e):
+        rows = 2 * wh * w.shape[2]
+        wv = jnp.concatenate(
+            [w[slab, part * (wb // 2) + last * wh:part * (wb // 2) + (last + 1) * wh] for part in range(2)],
+            axis=0,
+        ).reshape(rows, basis)
+        wv = jnp.concatenate([wv, wv], axis=0)
+        out = None
+        for f in range(2):
+            img = jnp.concatenate(
+                [image(last_rows(slab, part), wh, 4 * f + 2 * core, 2) for part in range(2)]
+                + [
+                    jnp.concatenate(
+                        [xs[e, part, f, :, c].reshape(rows // 2, quarter) for c in range(2)], axis=1
+                    )
+                    for part in range(2)
+                ],
+                axis=0,
+            )
+            term = lax.dot_general(wv, img, dims, preferred_element_type=jnp.float32)
+            out = term if out is None else out + term
+        return out.reshape(t1.shape[:3] + (2 * quarter,))
+
+    w_arrived(last)
+    out = last_product(q2, core)
+    t2[...] += out[:, :, :, quarter:]
+    t1[...] += out[:, :, :, :quarter]
+    w_forwarded(last)
+    out = last_product(qs2, 1 - core)
+    t2[...] += out[:, :, :, quarter:]
+    t1[...] += out[:, :, :, :quarter]
 
     def scatter(src, dst, ssem, rsem):
         for j in range(1, pairs):
@@ -281,11 +331,7 @@
     xi = par * 2 + xh
     xis = [(1 - par) * 2 + xh, (1 - par) * 2 + (1 - xh), par * 2 + (1 - xh)]
     row = [dev_a, dev_b, dev_d]
-    arrived(r0.at[1], qr_sem.at[1])
-    t2[...] = acc[:, :, :, pl.ds(mine + quarter, quarter)] + r0[1]
     scatter(t2, ry, qs_sem.at[5], qr_sem.at[5])
-    arrived(r0.at[0], qr_sem.at[0])
-    t1[...] = acc[:, :, :, pl.ds(mine, quarter)] + r0[0]
     for e in range(3):
         send(t1.at[:, xis[e]], rx.at[e], qs_sem.at[2 + e], qr_sem.at[2 + e], row[e])
     for e in range(3):
@@ -336,13 +382,11 @@
         out_specs=pl.BlockSpec(memory_space=pltpu.VMEM),
         scratch_shapes=[
             pltpu.VMEM((nb, slots, block, block), bf16),
-            pltpu.VMEM((4, 2 * nb + EARLY * cb, block, quarter), bf16),
+            pltpu.VMEM((4, 3 * nb, block, quarter), bf16),
             pltpu.VMEM((4, MIDDLE * cb, block, quarter), bf16),
             pltpu.VMEM((4, (CHUNKS - EARLY - MIDDLE) * cb, block, quarter), bf16),
             pltpu.VMEM((4, wb, block, basis), bf16),
             pltpu.VMEM((2, HALF_CHUNKS, wh, block, basis), bf16),
-            pltpu.VMEM((nb, block, basis), bf16),
-            pltpu.VMEM((nb, block, basis), bf16),
             pltpu.VMEM((pairs, 4, group, basis), f32),
             pltpu.VMEM((2, pairs, 4, group, quarter), f32),
             pltpu.VMEM((pairs, 4, group, quarter), f32),
@@ -355,10 +399,12 @@
             pltpu.VMEM((pairs - 1, group, quarter), f32),
             pltpu.VMEM((group, 2 * quarter), f32),
             pltpu.VMEM((group, 2 * quarter), f32),
-            dma((3,)),
+            pltpu.VMEM((2, 2, 2, wh, 2, block, quarter), bf16),
+            dma((5,)),
             dma((5, CHUNKS)), dma((5, CHUNKS)),
             dma((6, CHUNKS)), dma((6, CHUNKS)),
             dma((1 + 6 * HALF_CHUNKS,)), dma((1 + 6 * HALF_CHUNKS,)),
+            dma((8,)), dma((8,)),
             dma((11,)), dma((11,)),
         ],
         compiler_params=pltpu.CompilerParams(

time: 120 us -> 119 us (level)
    pallas_call x1, Pallas kernels: 119 us -> 118 us  [shards(): pl.pallas_call(functools.partial(kernel, regions), out_shape=jax.ShapeDty...]
where the time goes in v4:
time: 119 us
  Pallas kernels  118 us (99%)
  local copies, waits for them, and re-layouts  1.3 us (1%)
    pallas_call x1, Pallas kernels, shards(): pl.pallas_call(functools.partial(kernel, regions), out_shape=jax.ShapeDty...  118 us

profile of v4, /device:TPU:1, one launch (start us, length us, event | category | flops | bytes accessed | tf_op | source)
XLA Modules:
  0.0 118.8 jit_solution(15507699542784416225)
XLA Ops:
  0.0 117.5 %project.1 = f32[4,512]{1,0:T(4,128)} custom-call(s32[12,48]{1,0:T(8,128)} %bitcast.5, bf16[48,12,128,128]{3,2,1,0:T(8,128)(2,1)} %a_hbm.1, bf16[48,128,128]{2,1,0:T(8,128)(2,1)} %bitcast.3, bf16[12,128,512]{2,1,0:T(8,128)(2,1)} %bitcast.4), custom_call_target="tpu_custom_call" | custom-call | tf_op jit(solution)/shard_map/project/pallas_call | solution.py:378
  117.5 1.3 %copy.6 = f32[4,512]{1,0:T(4,128)} copy(f32[4,512]{1,0:T(4,128)} %project.1) | data formatting | bytes 16384

commit v5 on v4

--- a/solution.py
+++ b/solution.py
@@ -211,6 +211,19 @@
     at2 = par * (2 * nb + (EARLY + MIDDLE) * cb)
     put1 = pltpu.make_async_copy(y1, v.at[:, pl.ds(at1, MIDDLE * cb)], loc.at[3])
     put2 = pltpu.make_async_copy(y2, v.at[:, pl.ds(at2, (n - EARLY - MIDDLE) * cb)], loc.at[4])
+
+    def w_arrived(h):
+        for part in range(2):
+            o = 1 + (2 + part) * HALF_CHUNKS + h
+            ref = w.at[q2, pl.ds(part * (wb // 2) + h * wh, wh)]
+            arrived(ref, wrecv.at[o])
+            p = o + 2 * HALF_CHUNKS
+            send(ref, ref, ws.at[p], wrecv.at[p], dev_s)
+
+    def w_forwarded(h):
+        for part in range(2):
+            p = 1 + (4 + part) * HALF_CHUNKS + h
+            arrived(w.at[qs2, pl.ds(part * (wb // 2) + h * wh, wh)], wrecv.at[p])
 
     all_far(0, EARLY)
     image_rows(0)
@@ -231,10 +244,11 @@
     image_rows(5)
     relay_w(2)
     image_rows(6)
+    acc[...] += own_part([1, 2])
     take_far(7)
     all_far(EARLY + MIDDLE, n)
     put2.start()
-    acc[...] += own_part([1, 2])
+    w_arrived(0)
     put2.wait()
     image_rows(7)
 
@@ -258,24 +272,11 @@
         ats = [part * (wb // 2) + h * wh for part in range(2)]
         return product([(slab * wb + at, wh, w[slab, at:at + wh]) for at in ats])
 
-    def w_arrived(h):
-        for part in range(2):
-            o = 1 + (2 + part) * HALF_CHUNKS + h
-            ref = w.at[q2, pl.ds(part * (wb // 2) + h * wh, wh)]
-            arrived(ref, wrecv.at[o])
-            p = o + 2 * HALF_CHUNKS
-            send(ref, ref, ws.at[p], wrecv.at[p], dev_s)
-
-    def w_forwarded(h):
-        for part in range(2):
-            p = 1 + (4 + part) * HALF_CHUNKS + h
-            arrived(w.at[qs2, pl.ds(part * (wb // 2) + h * wh, wh)], wrecv.at[p])
-
+    for h in range(1, last):
+        w_arrived(h)
     for h in range(last):
-        w_arrived(h)
-        acc[...] += both(q2, h)
         w_forwarded(h)
-        acc[...] += both(qs2, h)
+        acc[...] += both(q2, h) + both(qs2, h)
 
     for e in (1, 0):
         cut = acc.at[:, :, :, pl.ds(theirs + e * quarter, quarter)]

time: 119 us -> 118 us (level)
  Pallas kernels: 118 us -> 116 us
where the time goes in v5:
time: 118 us
  Pallas kernels  116 us (98%)
  local copies, waits for them, and re-layouts  1.3 us (1%)
    pallas_call x1, Pallas kernels, shards(): pl.pallas_call(functools.partial(kernel, regions), out_shape=jax.ShapeDty...  116 us

profile of v5, /device:TPU:1, one launch (start us, length us, event | category | flops | bytes accessed | tf_op | source)
XLA Modules:
  0.0 117.8 jit_solution(7168876368652482421)
XLA Ops:
  0.0 116.5 %project.1 = f32[4,512]{1,0:T(4,128)} custom-call(s32[12,48]{1,0:T(8,128)} %bitcast.5, bf16[48,12,128,128]{3,2,1,0:T(8,128)(2,1)} %a_hbm.1, bf16[48,128,128]{2,1,0:T(8,128)(2,1)} %bitcast.3, bf16[12,128,512]{2,1,0:T(8,128)(2,1)} %bitcast.4), custom_call_target="tpu_custom_call" | custom-call | tf_op jit(solution)/shard_map/project/pallas_call | solution.py:379
  116.5 1.3 %copy.6 = f32[4,512]{1,0:T(4,128)} copy(f32[4,512]{1,0:T(4,128)} %project.1) | data formatting | bytes 16384

commit v6 on v5

--- a/solution.py
+++ b/solution.py
@@ -270,13 +270,13 @@
 
     def both(slab, h):
         ats = [part * (wb // 2) + h * wh for part in range(2)]
-        return product([(slab * wb + at, wh, w[slab, at:at + wh]) for at in ats])
+        return [(slab * wb + at, wh, w[slab, at:at + wh]) for at in ats]
 
     for h in range(1, last):
         w_arrived(h)
     for h in range(last):
         w_forwarded(h)
-        acc[...] += both(q2, h) + both(qs2, h)
+        acc[...] += product(both(q2, h) + both(qs2, h))
 
     for e in (1, 0):
         cut = acc.at[:, :, :, pl.ds(theirs + e * quarter, quarter)]

time: 118 us -> 118 us (level)
  no operation moved by 1% of the time
where the time goes in v6:
time: 118 us
  Pallas kernels  117 us (99%)
  local copies, waits for them, and re-layouts  1.3 us (1%)
    pallas_call x1, Pallas kernels, shards(): pl.pallas_call(functools.partial(kernel, regions), out_shape=jax.ShapeDty...  117 us

profile of v6, /device:TPU:1, one launch (start us, length us, event | category | flops | bytes accessed | tf_op | source)
XLA Modules:
  0.0 117.8 jit_solution(15406330332382630550)
XLA Ops:
  0.0 116.5 %project.1 = f32[4,512]{1,0:T(4,128)} custom-call(s32[12,48]{1,0:T(8,128)} %bitcast.5, bf16[48,12,128,128]{3,2,1,0:T(8,128)(2,1)} %a_hbm.1, bf16[48,128,128]{2,1,0:T(8,128)(2,1)} %bitcast.3, bf16[12,128,512]{2,1,0:T(8,128)(2,1)} %bitcast.4), custom_call_target="tpu_custom_call" | custom-call | tf_op jit(solution)/shard_map/project/pallas_call | solution.py:379
  116.5 1.3 %copy.6 = f32[4,512]{1,0:T(4,128)} copy(f32[4,512]{1,0:T(4,128)} %project.1) | data formatting | bytes 16384
